TPU v7x, 256 devices: a whole 4x4x8 slice. The times are simulated.
256 devices in a mesh: row: 16 (over y, x), col: 16 (over z, core).
Axes of the slice: x: 4, y: 4, z: 8, core: 2. Of those that a mesh axis runs over, the one named last changes fastest.
Arguments:
- fitting: bfloat16 [512, 512, 256], P(('row', 'col')), may hold values from -6 to 6
- coefficients: bfloat16 [64, 64, 6, 256, 128], P('row', 'col'), may hold values from -0.375 to 0.375
- amplitudes: bfloat16 [64, 64, 4096], P('row', 'col'), may hold values from -6 to 6
- intersections: bfloat16 [64, 64, 8, 4096], P('row', 'col'), may hold values from -0.33 to 1.33
- virtual_energy: float32 [64, 64, 64], P('row', 'col'), may hold values from 0.2 to 2
- occupied_energy: float32 [64], replicated, may hold values from -1.5 to -0.3
- kept_count: int32 [64, 64], P('row', 'col'), may hold values from 16 to 64
- orbital_atoms: int32 [64, 3], replicated, may hold values from 0 to 511, as said below
- fock_partner: int32 [64, 4], replicated, may hold values from 0 to 63, as said below
- fock_value: float32 [64, 4], replicated, may hold values from -3 to 3
Outputs:
- residual: float32 [64, 64, 4096], P('row', 'col')
Inputs may be any that keep to these rules, and one draw needn't show every extreme that they name: `orbital_atoms`: the 3 atoms of orbital i are different and lie in [(i // 4) * 32, (i // 4 + 1) * 32). fock_partner[i, n] differs from i by at most 4.
All inputs are finite; a program needn't handle non-finite values.
Results may differ from a plain program's by a relative error of at most 0.0029.
Values may be sent and summed in bfloat16 or wider, within the bound.
A program may use at most 128 MiB of HBM per device.

v0:
```python
import jax
import jax.numpy as jnp
from jax import lax
from jax.sharding import PartitionSpec as P

AUX = 512
NPNO = 64
DOMAIN = 3
PARTNERS = 4


def from_root(value, axis, source):
    kept = jnp.where(lax.axis_index(axis) == source, value, 0).astype(value.dtype)
    return lax.psum(kept, axis)


def passed_along(block, axis, distance):
    devices = range(lax.axis_size(axis))
    route = [(i - distance, i) for i in devices if i - distance in devices]
    return lax.ppermute(block, axis, route)


def on_device(
    fitting,
    coefficients,
    amplitudes,
    intersections,
    virtual_energy,
    occupied_energy,
    kept_count,
    orbital_atoms,
    fock_partner,
    fock_value,
):
    row_count = amplitudes.shape[0]
    column_count = amplitudes.shape[1]
    domain_size = orbital_atoms.shape[1]
    row_place = lax.axis_index("row")
    column_place = lax.axis_index("col")
    row_atoms = fitting.shape[0] * lax.axis_size("col")
    first_row = row_place * row_count
    first_column = column_place * column_count
    wanted = (
        lax.dynamic_slice_in_dim(orbital_atoms, first_row, row_count, 0) - row_place * row_atoms
    )
    piece = lax.all_gather(fitting, "col", axis=0, tiled=True)
    labels = jnp.arange(piece.shape[0], dtype=jnp.int32)
    picker = (wanted[:, :, None] == labels[None, None, :]).astype(jnp.bfloat16)
    added = jnp.einsum("ism,map->isap", picker, piece, preferred_element_type=jnp.float32)
    row_fit = added.astype(jnp.bfloat16)
    source_row = first_column // row_count
    column_fit = from_root(row_fit, "row", source_row)
    own_side = jnp.einsum(
        "isap,ijspq->ijsaq",
        row_fit,
        coefficients[:, :, :domain_size],
        preferred_element_type=jnp.float32,
    ).astype(jnp.bfloat16)
    other_side = jnp.einsum(
        "jsap,ijspq->ijsaq",
        column_fit,
        coefficients[:, :, domain_size:],
        preferred_element_type=jnp.float32,
    ).astype(jnp.bfloat16)
    exchange_part = jnp.einsum(
        "ijsaq,ijsar->ijqr",
        own_side[..., :NPNO],
        own_side[..., NPNO:],
        preferred_element_type=jnp.float32,
    )
    exchange_part = exchange_part + jnp.einsum(
        "ijsaq,ijsar->ijqr",
        other_side[..., :NPNO],
        other_side[..., NPNO:],
        preferred_element_type=jnp.float32,
    )
    exchange_part = exchange_part * (2 * DOMAIN * AUX) ** (-0.5)
    row_partner = lax.dynamic_slice_in_dim(fock_partner, first_row, row_count, 0)
    column_partner = lax.dynamic_slice_in_dim(fock_partner, first_column, column_count, 0)
    below_rows = passed_along(amplitudes, "row", 1)
    above_rows = passed_along(amplitudes, "row", -1)
    row_source = jnp.concatenate([below_rows, amplitudes, above_rows], axis=0)
    below_columns = passed_along(amplitudes, "col", 1)
    above_columns = passed_along(amplitudes, "col", -1)
    column_source = jnp.concatenate([below_columns, amplitudes, above_columns], axis=1)
    row_pick = row_partner - (first_row - column_count)
    column_pick = column_partner - (first_column - column_count)
    from_rows = jnp.transpose(jnp.take(row_source, row_pick, axis=0), (0, 2, 1, 3))
    from_columns = jnp.take(column_source, column_pick, axis=1)
    partners = jnp.concatenate([from_rows, from_columns], axis=2).reshape(
        row_count, column_count, 2 * PARTNERS, NPNO, NPNO
    )
    intersection_mats = intersections.reshape(row_count, column_count, 2 * PARTNERS, NPNO, NPNO)
    half = jnp.einsum(
        "ijnab,ijnbc->ijnac", intersection_mats, partners, preferred_element_type=jnp.float32
    ).astype(jnp.bfloat16)
    sandwich = jnp.einsum(
        "ijnac,ijndc->ijnad", half, intersection_mats, preferred_element_type=jnp.float32
    )
    row_weight = lax.dynamic_slice_in_dim(fock_value, first_row, row_count, 0)
    column_weight = lax.dynamic_slice_in_dim(fock_value, first_column, column_count, 0)
    weights = jnp.concatenate(
        [
            jnp.broadcast_to(row_weight[:, None, :], (row_count, column_count, PARTNERS)),
            jnp.broadcast_to(column_weight[None, :, :], (row_count, column_count, PARTNERS)),
        ],
        axis=2,
    )
    coupling = jnp.einsum("ijn,ijnad->ijad", weights, sandwich)
    row_occupied = lax.dynamic_slice_in_dim(occupied_energy, first_row, row_count, 0)
    column_occupied = lax.dynamic_slice_in_dim(occupied_energy, first_column, column_count, 0)
    shift = (
        virtual_energy[:, :, :, None]
        + virtual_energy[:, :, None, :]
        - row_occupied[:, None, None, None]
        - column_occupied[None, :, None, None]
    )
    current = amplitudes.reshape(row_count, column_count, NPNO, NPNO).astype(jnp.float32)
    result = exchange_part + shift * current - coupling
    levels = jnp.arange(NPNO, dtype=jnp.int32)
    count = kept_count[:, :, None, None]
    keep = (levels[None, None, :, None] < count) & (levels[None, None, None, :] < count)
    masked = jnp.where(keep, result, jnp.zeros_like(result))
    return masked.reshape(row_count, column_count, NPNO * NPNO)


def solution(mesh):
    placed = (
        P(("row", "col"), None, None),
        P("row", "col", None, None, None),
        P("row", "col", None),
        P("row", "col", None, None),
        P("row", "col", None),
        P(),
        P("row", "col"),
        P(),
        P(),
        P(),
    )
    return jax.shard_map(
        on_device, mesh=mesh, in_specs=placed, out_specs=P("row", "col", None), check_vma=False
    )
```

profile of v0, /device:TPU:1, one launch (start us, length us, event | category | flops | bytes accessed | tf_op | source)
XLA Modules:
  0.0 198.9 jit_solution(497864777100827050)
XLA Ops:
  6.5 0.0 all-gather.2.cloned.1.call-start
  6.5 0.7 all-gather.2.cloned.1.call-update
  7.3 0.0 all-reduce.2.cloned.1.call-start
  7.3 1.0 copy.82
  8.3 4.9 %collective-permute-start.2 = (bf16[4,4,4096]{2,0,1:T(4,128)(2,1)S(1)}, bf16[4,4,4096]{2,0,1:T(4,128)(2,1)S(1)}, u32[]{:S(2)}, u32[]{:S(2)}) collective-permute-start(bf16[4,4,4096]{2,0,1:T(4,128)(2,1)S(1)} %copy.82), channel_id=1, source_target_pairs={{0,1},{1,2},{2,3},{3,4},{4,5},{5,6},{6,7},{7,8},{8,9},{9,10},{10,1... | collective-permute-start | bytes 393224 | tf_op jit(solution)/shard_map/ppermute | solution.py:20
  13.2 1.9 collective-permute-start.3
  15.2 3.1 %collective-permute-start = (bf16[4,4,4096]{2,1,0:T(4,128)(2,1)}, bf16[4,4,4096]{2,1,0:T(4,128)(2,1)S(1)}, u32[]{:S(2)}, u32[]{:S(2)}) collective-permute-start(bf16[4,4,4096]{2,1,0:T(4,128)(2,1)} %param.12), channel_id=1, source_target_pairs={{0,16},{16,32},{32,48},{48,64},{64,80},{80,96},{96,112},{112,128},... | collective-permute-start | bytes 393224 | tf_op jit(solution)/shard_map/ppermute | solution.py:20
  18.3 1.3 collective-permute-start.1
  19.6 0.8 compare_and_fusion.1
  20.5 0.1 copy.85
  20.6 0.1 reshape.58
  20.6 0.1 copy.79
  20.7 0.1 reshape.50
  20.8 0.8 dynamic-slice_subtract_fusion
  21.6 0.8 constant_dynamic-slice_fusion.1
  22.4 0.8 iota_compare_fusion
  23.2 0.0 copy-start.4
  23.2 0.0 copy-start.1
  23.2 6.7 %fusion.63 = (bf16[4,4,3,256,128]{4,3,2,1,0:T(8,128)(2,1)}, bf16[4,4,3,256,128]{4,3,2,1,0:T(8,128)(2,1)}) fusion(bf16[4,4,6,256,128]{4,3,2,1,0:T(8,128)(2,1)} %param.11), kind=kLoop, calls=%fused_computation.53 | loop fusion | bytes 12582912 | tf_op jit(solution)/shard_map/slice | solution.py:62
  29.9 0.0 copy-done.4
  29.9 0.1 fusion.65
  30.0 0.0 copy-done.1
  30.0 1.0 reshape.47
  31.1 0.1 copy.81
  31.2 0.1 copy.78
  31.3 3.3 %reshape.45 = bf16[4,4,8,64,64]{4,3,2,1,0:T(8,128)(2,1)S(1)} reshape(bf16[4,4,8,4096]{3,2,1,0:T(8,128)(2,1)} %param.13) | data formatting | bytes 2097152 | tf_op jit(solution)/shard_map/reshape | solution.py:93
  34.5 0.1 copy.76
  34.6 0.1 copy.77
  34.7 0.1 pad_maximum_fusion.3
  34.8 0.0 collective-permute-done.2
  34.8 0.0 collective-permute-done.3
  34.8 0.3 pad_maximum_fusion.2
  35.1 1.0 gather_fusion.1
  36.1 0.0 collective-permute-done
  36.1 0.0 collective-permute-done.1
  36.1 0.3 pad_maximum_fusion.1
  36.4 1.8 gather_fusion
  38.2 1.5 fusion.57
  39.7 29.6 %all-gather.2.cloned.1.call-done = bf16[32,512,256]{2,1,0:T(8,128)(2,1)} async-done(((bf16[2,512,256]{2,1,0:T(8,128)(2,1)}), bf16[32,512,256]{2,1,0:T(8,128)(2,1)}) %all-gather.2.cloned.1.call-update) | async-done | bytes 8388624 | tf_op jit(solution)/shard_map/all_gather | solution.py:46
  69.2 12.0 %broadcast_select_fusion = (bf16[4,3,512,256]{3,0,2,1:T(4,128)(2,1)}, bf16[4,3,512,256]{3,0,2,1:T(4,128)(2,1)}) fusion(pred[]{:T(512)S(6)} %eq.19, bf16[32,512,256]{2,1,0:T(8,128)(2,1)} %all-gather.2.cloned.1.call-done, s32[4,3]{0,1:T(4,128)S(1)} %dynamic-slice_subtract_fusion), kind=kOutput, calls=%fused_computation.19 | convolution fusion | flops 103809408 | bytes 14680113 | tf_op jit(solution)/shard_map/ism,map->isap/dot_general | solution.py:49
  81.2 0.0 all-reduce.2.cloned.1.call-update
  81.2 2.0 pad_maximum_fusion
  83.2 3.3 %reshape.44 = bf16[4,4,8,64,64]{4,3,2,1,0:T(8,128)(2,1)} reshape(bf16[4,4,8,4096]{3,2,1,0:T(8,128)(2,1)S(1)} %pad_maximum_fusion) | data formatting | bytes 2097152 | tf_op jit(solution)/shard_map/reshape | solution.py:90
  86.5 5.3 %fusion.18 = bf16[4,4,8,64,64]{4,3,2,1,0:T(8,128)(2,1)} fusion(bf16[4,4,8,64,64]{4,3,2,1,0:T(8,128)(2,1)S(1)} %reshape.45, bf16[4,4,8,64,64]{4,3,2,1,0:T(8,128)(2,1)} %reshape.44), kind=kOutput, calls=%fused_computation.21 | convolution fusion | flops 134742016 | bytes 3145728 | tf_op jit(solution)/shard_map/ijnac,ijndc->ijnad/dot_general | solution.py:97
  91.8 3.8 %fusion.3 = f32[4,4,1,64,64]{4,2,3,1,0:T(1,128)} fusion(f32[4,4,8,1,1]{2,3,4,1,0:T(1,128)S(1)} %bitcast.64, bf16[4,4,8,64,64]{4,3,2,1,0:T(8,128)(2,1)} %fusion.18), kind=kOutput, calls=%fused_computation.7 | convolution fusion | flops 1048576 | bytes 1311232 | tf_op jit(solution)/shard_map/ijn,ijnad->ijad/dot_general | solution.py:109
  95.6 4.8 %convert_bitcast_fusion.1 = bf16[4,4,3,512,128]{3,4,1,2,0:T(8,128)(2,1)S(1)} fusion(bf16[4,4,3,256,128]{4,3,2,1,0:T(8,128)(2,1)} %get-tuple-element.12, bf16[4,3,512,256,1]{3,0,2,1,4:T(4,128)(2,1)} %bitcast.60), kind=kOutput, calls=%fused_computation.6 | convolution fusion | flops 1613758464 | bytes 12582912 | tf_op jit(solution)/shard_map/isap,ijspq->ijsaq/dot_general | solution.py:53
  100.4 0.8 fusion.64
  101.2 0.0 copy-start
  101.2 1.7 fusion.22
  103.0 82.1 %all-reduce.2.cloned.1.call-done = bf16[4,3,512,256]{3,0,2,1:T(4,128)(2,1)} async-done(((bf16[4,3,512,256]{3,0,2,1:T(4,128)(2,1)}), bf16[4,3,512,256]{3,0,2,1:T(4,128)(2,1)}) %all-reduce.2.cloned.1.call-update) | async-done | bytes 3145744 | tf_op jit(solution)/shard_map/psum | solution.py:14
  185.0 0.0 copy-done
  185.1 3.7 %convert_bitcast_fusion = bf16[4,4,3,512,128]{3,4,0,2,1:T(8,128)(2,1)S(1)} fusion(bf16[4,4,3,256,128]{4,3,2,1,0:T(8,128)(2,1)S(1)} %copy-done, bf16[4,3,512,256,1]{3,0,2,1,4:T(4,128)(2,1)} %bitcast.59), kind=kOutput, calls=%fused_computation.5 | convolution fusion | flops 1613758464 | bytes 12582912 | tf_op jit(solution)/shard_map/jsap,ijspq->ijsaq/dot_general | solution.py:59
  188.8 0.0 copy-start.2
  188.8 0.0 copy-start.3
  188.8 0.0 copy-start.5
  188.8 0.0 copy-start.6
  188.8 0.4 fusion.62
  189.3 0.5 copy-done.2
  189.8 0.2 copy-done.3
  190.0 0.0 copy-done.5
  190.0 0.2 copy-done.6
  190.2 1.0 fusion.52
  191.2 0.9 reshape.46
  (4 shorter events, 0.0 us)
Async XLA Ops:
  6.5 62.7 %all-gather.2.cloned.1.call-start = ((), (), s32[]{:S(2)}) async-start(), calls=%async_computation | async-start | bytes 8912896 | tf_op jit(solution)/shard_map/all_gather | solution.py:46
  7.3 177.8 %all-reduce.2.cloned.1.call-start = ((), (), s32[]{:S(2)}) async-start(), calls=%async_computation.1 | async-start | bytes 6291456 | tf_op jit(solution)/shard_map/psum | solution.py:14
  8.3 26.5 %collective-permute-start.2 = (bf16[4,4,4096]{2,0,1:T(4,128)(2,1)S(1)}, bf16[4,4,4096]{2,0,1:T(4,128)(2,1)S(1)}, u32[]{:S(2)}, u32[]{:S(2)}) collective-permute-start(bf16[4,4,4096]{2,0,1:T(4,128)(2,1)S(1)} %copy.82), channel_id=1, source_target_pairs={{0,1},{1,2},{2,3},{3,4},{4,5},{5,6},{6,7},{7,8},{8,9},{9,10},{10,1... | collective-permute-start | bytes 393224 | tf_op jit(solution)/shard_map/ppermute | solution.py:20
  13.2 21.6 %collective-permute-start.3 = (bf16[4,4,4096]{2,0,1:T(4,128)(2,1)S(1)}, bf16[4,4,4096]{2,0,1:T(4,128)(2,1)S(1)}, u32[]{:S(2)}, u32[]{:S(2)}) collective-permute-start(bf16[4,4,4096]{2,0,1:T(4,128)(2,1)S(1)} %copy.82), channel_id=1, source_target_pairs={{1,0},{2,1},{3,2},{4,3},{5,4},{6,5},{7,6},{8,7},{9,8},{10,9},{11,1... | collective-permute-start | bytes 393224 | tf_op jit(solution)/shard_map/ppermute | solution.py:20
  15.2 20.9 %collective-permute-start = (bf16[4,4,4096]{2,1,0:T(4,128)(2,1)}, bf16[4,4,4096]{2,1,0:T(4,128)(2,1)S(1)}, u32[]{:S(2)}, u32[]{:S(2)}) collective-permute-start(bf16[4,4,4096]{2,1,0:T(4,128)(2,1)} %param.12), channel_id=1, source_target_pairs={{0,16},{16,32},{32,48},{48,64},{64,80},{80,96},{96,112},{112,128},... | collective-permute-start | bytes 393224 | tf_op jit(solution)/shard_map/ppermute | solution.py:20
  18.3 17.8 %collective-permute-start.1 = (bf16[4,4,4096]{2,1,0:T(4,128)(2,1)}, bf16[4,4,4096]{2,1,0:T(4,128)(2,1)S(1)}, u32[]{:S(2)}, u32[]{:S(2)}) collective-permute-start(bf16[4,4,4096]{2,1,0:T(4,128)(2,1)} %param.12), channel_id=1, source_target_pairs={{16,0},{32,16},{48,32},{64,48},{80,64},{96,80},{112,96},{128,112},... | collective-permute-start | bytes 393224 | tf_op jit(solution)/shard_map/ppermute | solution.py:20
  23.2 6.8 %copy-start.4 = (f32[64]{0:T(128)S(1)}, f32[64]{0:T(128)}, u32[]{:S(2)}) copy-start(f32[64]{0:T(128)} %param.15) | copy-start | bytes 772
  23.2 6.8 %copy-start.1 = (bf16[4,4,4096]{2,1,0:T(4,128)(2,1)S(1)}, bf16[4,4,4096]{2,1,0:T(4,128)(2,1)}, u32[]{:S(2)}) copy-start(bf16[4,4,4096]{2,1,0:T(4,128)(2,1)} %param.12) | copy-start | bytes 393220
  101.2 83.8 %copy-start = (bf16[4,4,3,256,128]{4,3,2,1,0:T(8,128)(2,1)S(1)}, bf16[4,4,3,256,128]{4,3,2,1,0:T(8,128)(2,1)}, u32[]{:S(2)}) copy-start(bf16[4,4,3,256,128]{4,3,2,1,0:T(8,128)(2,1)} %get-tuple-element.11) | copy-start | bytes 9437188
  188.8 1.0 copy-start.2
  188.8 1.2 copy-start.3
  188.8 1.2 copy-start.5
  188.8 1.3 copy-start.6
Sparse Core Ops, SparseCore 0:
  9.2 60.0 all-gather.1
  81.4 103.6 all-reduce.1
where the time goes:
time: 199 us
  waiting for transfers between devices  112 us (56%)
  matrix products  32.4 us (16%)
  local copies, waits for them, and re-layouts  22.8 us (11%)
  between operations  13.6 us (7%)
  starting transfers between devices  11.3 us (6%)
  other arithmetic  6.46 us (3%)
    psum x1, waiting for transfers between devices, from_root(): return lax.psum(kept, axis)  82.1 us
    all_gather x1, waiting for transfers between devices, on_device(): piece = lax.all_gather(fitting, 'col', axis=0, tiled=True)  29.6 us
    dot_general x1, matrix products, on_device(): jnp.einsum('ism,map->isap', picker, piece, preferred_element_type=jnp.flo...  12 us
    ppermute x4, starting transfers between devices, passed_along(): return lax.ppermute(block, axis, route)  11.3 us
    slice x1, local copies, waits for them, and re-layouts, on_device(): coefficients[:, :, domain_size:]  6.75 us
    dot_general x1, matrix products, on_device(): jnp.einsum('ijnac,ijndc->ijnad', half, intersection_mats, preferred_eleme...  5.3 us
    dot_general x1, matrix products, on_device(): jnp.einsum('isap,ijspq->ijsaq', row_fit, coefficients[:, :, :domain_size]...  4.82 us
  transfers between devices with their start and end apart: 6, of which 2 were waited for; matrix products, arithmetic and copies ran while one was open for 21% of the time, Pallas kernels for 0%

commit v1 on v0

--- a/solution.py
+++ b/solution.py
@@ -43,7 +43,9 @@
     wanted = (
         lax.dynamic_slice_in_dim(orbital_atoms, first_row, row_count, 0) - row_place * row_atoms
     )
-    piece = lax.all_gather(fitting, "col", axis=0, tiled=True)
+    piece = jnp.concatenate(
+        lax.all_to_all(jnp.stack([fitting for _ in range(lax.axis_size("col"))], 0), "col", 0, 0), 0
+    )
     labels = jnp.arange(piece.shape[0], dtype=jnp.int32)
     picker = (wanted[:, :, None] == labels[None, None, :]).astype(jnp.bfloat16)
     added = jnp.einsum("ism,map->isap", picker, piece, preferred_element_type=jnp.float32)

time: 199 us -> 368 us (1.85)
  waiting for transfers between devices: 112 us -> 246 us
  local copies, waits for them, and re-layouts: 22.8 us -> 54 us
  starting transfers between devices: 11.3 us -> 20 us
    ppermute x4, waiting for transfers between devices: 0.01 us -> 162 us  [passed_along(): return lax.ppermute(block, axis, route)]
    all_gather x1 -> x0, waiting for transfers between devices: 29.6 us -> none  [on_device(): piece = lax.all_gather(fitting, 'col', axis=0, tiled=True)]
    reshape x0 -> x1, local copies, waits for them, and re-layouts: none -> 13.1 us  [on_device(): jnp.concatenate(lax.all_to_all(jnp.stack([fitting for _ in range(lax.axis...]
    all_to_all x0 -> x1, local copies, waits for them, and re-layouts: none -> 10.9 us  [on_device(): lax.all_to_all(jnp.stack([fitting for _ in range(lax.axis_size('col'))],...]
    all_to_all x0 -> x1, starting transfers between devices: none -> 10.1 us  [on_device(): lax.all_to_all(jnp.stack([fitting for _ in range(lax.axis_size('col'))],...]
    another operation x0 -> x1, local copies, waits for them, and re-layouts: none -> 7.61 us  [on_device(): jnp.stack([fitting for _ in range(lax.axis_size('col'))], 0)]
  transfers between devices with their start and end apart: 6 -> 6, of which waited for: 2 -> 3; matrix products, arithmetic and copies ran while one was open for 21% -> 11% of each run, Pallas kernels for 0% -> 0%
where the time goes in v1:
time: 368 us; the launch traced here: 367 us
  waiting for transfers between devices  246 us (67%)
  local copies, waits for them, and re-layouts  54 us (15%)
  matrix products  29.5 us (8%)
  starting transfers between devices  20 us (5%)
  between operations  13.6 us (4%)
  other arithmetic  4.34 us (1%)
    ppermute x4, waiting for transfers between devices, passed_along(): return lax.ppermute(block, axis, route)  162 us
    psum x1, waiting for transfers between devices, from_root(): return lax.psum(kept, axis)  83.6 us
    reshape x1, local copies, waits for them, and re-layouts, on_device(): jnp.concatenate(lax.all_to_all(jnp.stack([fitting for _ in range(lax.axis...  13.1 us
    all_to_all x1, local copies, waits for them, and re-layouts, on_device(): lax.all_to_all(jnp.stack([fitting for _ in range(lax.axis_size('col'))],...  10.9 us
    all_to_all x1, starting transfers between devices, on_device(): lax.all_to_all(jnp.stack([fitting for _ in range(lax.axis_size('col'))],...  10.1 us
    ppermute x4, starting transfers between devices, passed_along(): return lax.ppermute(block, axis, route)  9.88 us
    dot_general x1, matrix products, on_device(): jnp.einsum('ism,map->isap', picker, piece, preferred_element_type=jnp.flo...  8.78 us
    another operation x1, local copies, waits for them, and re-layouts, on_device(): jnp.stack([fitting for _ in range(lax.axis_size('col'))], 0)  7.61 us
  transfers between devices with their start and end apart: 6, of which 3 were waited for; matrix products, arithmetic and copies ran while one was open for 11% of the time, Pallas kernels for 0%

profile of v1, /device:TPU:1, one launch (start us, length us, event | category | flops | bytes accessed | tf_op | source)
XLA Modules:
  0.0 367.1 jit_solution(14670217610529385509)
XLA Ops:
  6.5 1.6 copy.68
  8.1 7.6 %stack.2 = bf16[16,2,512,256]{3,1,2,0:T(2,128)(2,1)} broadcast(bf16[2,512,256]{2,0,1:T(2,128)(2,1)S(1)} %copy.68), dimensions={1,2,3} | broadcast | bytes 8912896 | tf_op jit(solution)/shard_map/stack | solution.py:47
  15.7 0.0 copy-start.4
  15.7 0.0 copy-start.8
  15.8 10.1 %all-to-all-start = ((bf16[16,2,512,256]{3,1,2,0:T(2,128)(2,1)}), bf16[16,2,512,256]{3,1,2,0:T(2,128)(2,1)}, u32[]{:S(2)}, u32[]{:S(2)}) async-start(bf16[16,2,512,256]{3,1,2,0:T(2,128)(2,1)} %stack.2), calls=%async_computation | async-start | bytes 16777216 | tf_op jit(solution)/shard_map/all_to_all | solution.py:47
  25.9 0.0 all-reduce.2.cloned.1.call-start
  25.9 0.0 copy-done.1
  25.9 0.1 copy.84
  26.0 3.5 collective-permute-start.2
  29.6 1.9 collective-permute-start.3
  31.5 3.1 collective-permute-start
  34.6 1.3 collective-permute-start.1
  36.0 0.0 copy-done.5
  36.0 0.1 compare_and_fusion.1
  36.0 0.1 copy.87
  36.1 0.1 reshape.64
  36.2 0.1 copy.81
  36.3 0.1 reshape.56
  36.4 0.0 copy-done.7
  36.4 0.1 dynamic-slice_subtract_fusion
  36.5 0.1 constant_dynamic-slice_fusion.1
  36.6 0.0 copy-done.8
  36.6 0.1 iota_compare_fusion
  36.7 6.3 %fusion.57 = (bf16[4,4,3,256,128]{4,3,2,1,0:T(8,128)(2,1)}, bf16[4,4,3,256,128]{4,3,2,1,0:T(8,128)(2,1)}) fusion(bf16[4,4,6,256,128]{4,3,2,1,0:T(8,128)(2,1)} %param.11), kind=kLoop, calls=%fused_computation.50 | loop fusion | bytes 12582912 | tf_op jit(solution)/shard_map/slice | solution.py:64
  43.0 0.1 fusion.59
  43.1 1.0 reshape.53
  44.1 0.1 copy.83
  44.2 0.1 copy.80
  44.3 3.3 reshape.51
  47.6 0.1 copy.78
  47.7 0.1 copy.79
  47.8 0.1 pad_maximum_fusion.3
  47.9 160.1 %collective-permute-done.2 = bf16[4,4,4096]{2,0,1:T(4,128)(2,1)S(1)} collective-permute-done((bf16[4,4,4096]{2,0,1:T(4,128)(2,1)S(1)}, bf16[4,4,4096]{2,0,1:T(4,128)(2,1)S(1)}, u32[]{:S(2)}, u32[]{:S(2)}) %collective-permute-start.2) | collective-permute-done | bytes 131104 | tf_op jit(solution)/shard_map/ppermute | solution.py:20
  208.0 1.9 collective-permute-done.3
  209.8 0.3 pad_maximum_fusion.2
  210.1 1.0 gather_fusion.1
  211.1 0.0 collective-permute-done
  211.1 0.0 collective-permute-done.1
  211.1 0.3 pad_maximum_fusion.1
  211.4 1.8 gather_fusion
  213.2 1.5 fusion.51
  214.7 0.0 all-to-all-done
  214.7 10.9 %copy.69 = bf16[16,2,512,256]{3,1,0,2:T(2,128)(2,1)} copy(bf16[16,2,512,256]{3,1,2,0:T(2,128)(2,1)} %all-to-all-done) | data formatting | bytes 16777216 | tf_op jit(solution)/shard_map/all_to_all | solution.py:47
  225.6 13.1 %reshape.75 = bf16[32,512,256,1]{2,0,1,3:T(8,128)(2,1)} reshape(bf16[16,2,512,256]{3,1,0,2:T(2,128)(2,1)} %copy.69) | data formatting | bytes 16777216 | tf_op jit(solution)/shard_map/reshape | solution.py:46
  238.7 8.8 %broadcast_select_fusion = (bf16[4,3,512,256]{3,0,2,1:T(4,128)(2,1)}, bf16[4,3,512,256]{3,0,2,1:T(4,128)(2,1)}) fusion(pred[]{:T(512)S(6)} %eq.19, bf16[32,512,256,1]{2,0,1,3:T(8,128)(2,1)} %reshape.75, s32[4,3]{0,1:T(4,128)S(1)} %dynamic-slice_subtract_fusion), kind=kOutput, calls=%fused_computation.16 | convolution fusion | flops 103809408 | bytes 14680113 | tf_op jit(solution)/shard_map/ism,map->isap/dot_general | solution.py:51
  247.5 0.0 all-reduce.2.cloned.1.call-update
  247.5 2.0 pad_maximum_fusion
  249.5 3.3 reshape.50
  252.8 5.3 %fusion.12 = bf16[4,4,8,64,64]{4,3,2,1,0:T(8,128)(2,1)} fusion(bf16[4,4,8,64,64]{4,3,2,1,0:T(8,128)(2,1)S(1)} %reshape.51, bf16[4,4,8,64,64]{4,3,2,1,0:T(8,128)(2,1)} %reshape.50), kind=kOutput, calls=%fused_computation.18 | convolution fusion | flops 134742016 | bytes 3145728 | tf_op jit(solution)/shard_map/ijnac,ijndc->ijnad/dot_general | solution.py:99
  258.0 4.2 %fusion = f32[4,4,1,64,64]{4,2,3,1,0:T(1,128)} fusion(f32[4,4,8,1,1]{2,3,4,1,0:T(1,128)S(1)} %bitcast.60, bf16[4,4,8,64,64]{4,3,2,1,0:T(8,128)(2,1)} %fusion.12), kind=kOutput, calls=%fused_computation.4 | convolution fusion | flops 1048576 | bytes 1311232 | tf_op jit(solution)/shard_map/ijn,ijnad->ijad/dot_general | solution.py:111
  262.3 4.8 %convert_bitcast_fusion.1 = bf16[4,4,3,512,128]{3,4,1,2,0:T(8,128)(2,1)S(1)} fusion(bf16[4,4,3,256,128]{4,3,2,1,0:T(8,128)(2,1)} %get-tuple-element.12, bf16[4,3,512,256,1]{3,0,2,1,4:T(4,128)(2,1)} %bitcast.55), kind=kOutput, calls=%fused_computation.3 | convolution fusion | flops 1613758464 | bytes 12582912 | tf_op jit(solution)/shard_map/isap,ijspq->ijsaq/dot_general | solution.py:55
  267.1 0.8 fusion.58
  267.9 1.8 fusion.16
  269.6 83.6 %all-reduce.2.cloned.1.call-done = bf16[4,3,512,256]{3,0,2,1:T(4,128)(2,1)} async-done(((bf16[4,3,512,256]{3,0,2,1:T(4,128)(2,1)}), bf16[4,3,512,256]{3,0,2,1:T(4,128)(2,1)}) %all-reduce.2.cloned.1.call-update) | async-done | bytes 3145744 | tf_op jit(solution)/shard_map/psum | solution.py:14
  353.2 3.7 %convert_bitcast_fusion = bf16[4,4,3,512,128]{3,4,0,2,1:T(8,128)(2,1)S(1)} fusion(bf16[4,4,3,256,128]{4,3,2,1,0:T(8,128)(2,1)S(1)} %copy-done, bf16[4,3,512,256,1]{3,0,2,1,4:T(4,128)(2,1)} %bitcast.56), kind=kOutput, calls=%fused_computation.2 | convolution fusion | flops 1613758464 | bytes 12582912 | tf_op jit(solution)/shard_map/jsap,ijspq->ijsaq/dot_general | solution.py:61
  357.0 0.0 copy-start.2
  357.0 0.0 copy-start.3
  357.0 0.0 copy-start.9
  357.0 0.4 fusion.56
  357.5 0.5 copy-done.2
  358.0 0.2 copy-done.3
  358.2 0.2 copy-done.10
  358.4 1.0 fusion.46
  359.4 0.9 reshape.52
  (14 shorter events, 0.0 us)
Async XLA Ops:
  15.7 10.2 %copy-start.1 = (bf16[4,4,4096]{2,1,0:T(4,128)(2,1)S(1)}, bf16[4,4,4096]{2,1,0:T(4,128)(2,1)}, u32[]{:S(2)}) copy-start(bf16[4,4,4096]{2,1,0:T(4,128)(2,1)} %param.12) | copy-start | bytes 393220
  15.7 20.2 %copy-start.5 = (s32[64,4]{0,1:T(4,128)S(1)}, s32[64,4]{0,1:T(4,128)}, u32[]{:S(2)}) copy-start(s32[64,4]{0,1:T(4,128)} %param.18) | copy-start | bytes 3076
  15.7 20.7 %copy-start.7 = (s32[64,3]{0,1:T(4,128)S(1)}, s32[64,3]{0,1:T(4,128)}, u32[]{:S(2)}) copy-start(s32[64,3]{0,1:T(4,128)} %param.17) | copy-start | bytes 2308
  15.7 20.8 %copy-start.4 = (f32[64,4]{0,1:T(4,128)S(1)}, f32[64,4]{0,1:T(4,128)}, u32[]{:S(2)}) copy-start(f32[64,4]{0,1:T(4,128)} %param.19) | copy-start | bytes 3076
  15.7 20.8 %copy-start.8 = (s32[4,4]{1,0:T(4,128)S(1)}, s32[4,4]{1,0:T(4,128)}, u32[]{:S(2)}) copy-start(s32[4,4]{1,0:T(4,128)} %param.16) | copy-start | bytes 196
  15.8 198.9 %all-to-all-start = ((bf16[16,2,512,256]{3,1,2,0:T(2,128)(2,1)}), bf16[16,2,512,256]{3,1,2,0:T(2,128)(2,1)}, u32[]{:S(2)}, u32[]{:S(2)}) async-start(bf16[16,2,512,256]{3,1,2,0:T(2,128)(2,1)} %stack.2), calls=%async_computation | async-start | bytes 16777216 | tf_op jit(solution)/shard_map/all_to_all | solution.py:47
  25.9 327.4 %all-reduce.2.cloned.1.call-start = ((), (), s32[]{:S(2)}) async-start(), calls=%async_computation.1 | async-start | bytes 6291456 | tf_op jit(solution)/shard_map/psum | solution.py:14
  26.0 181.9 %collective-permute-start.2 = (bf16[4,4,4096]{2,0,1:T(4,128)(2,1)S(1)}, bf16[4,4,4096]{2,0,1:T(4,128)(2,1)S(1)}, u32[]{:S(2)}, u32[]{:S(2)}) collective-permute-start(bf16[4,4,4096]{2,0,1:T(4,128)(2,1)S(1)} %copy.84), channel_id=1, source_target_pairs={{0,1},{1,2},{2,3},{3,4},{4,5},{5,6},{6,7},{7,8},{8,9},{9,10},{10,1... | collective-permute-start | bytes 393224 | tf_op jit(solution)/shard_map/ppermute | solution.py:20
  29.6 180.3 %collective-permute-start.3 = (bf16[4,4,4096]{2,0,1:T(4,128)(2,1)S(1)}, bf16[4,4,4096]{2,0,1:T(4,128)(2,1)S(1)}, u32[]{:S(2)}, u32[]{:S(2)}) collective-permute-start(bf16[4,4,4096]{2,0,1:T(4,128)(2,1)S(1)} %copy.84), channel_id=1, source_target_pairs={{1,0},{2,1},{3,2},{4,3},{5,4},{6,5},{7,6},{8,7},{9,8},{10,9},{11,1... | collective-permute-start | bytes 393224 | tf_op jit(solution)/shard_map/ppermute | solution.py:20
  31.5 179.6 %collective-permute-start = (bf16[4,4,4096]{2,1,0:T(4,128)(2,1)S(1)}, bf16[4,4,4096]{2,1,0:T(4,128)(2,1)S(1)}, u32[]{:S(2)}, u32[]{:S(2)}) collective-permute-start(bf16[4,4,4096]{2,1,0:T(4,128)(2,1)S(1)} %copy-done.1), channel_id=1, source_target_pairs={{0,16},{16,32},{32,48},{48,64},{64,80},{80,96},{96,112},{112,128},... | collective-permute-start | bytes 393224 | tf_op jit(solution)/shard_map/ppermute | solution.py:20
  34.6 176.5 %collective-permute-start.1 = (bf16[4,4,4096]{2,1,0:T(4,128)(2,1)S(1)}, bf16[4,4,4096]{2,1,0:T(4,128)(2,1)S(1)}, u32[]{:S(2)}, u32[]{:S(2)}) collective-permute-start(bf16[4,4,4096]{2,1,0:T(4,128)(2,1)S(1)} %copy-done.1), channel_id=1, source_target_pairs={{16,0},{32,16},{48,32},{64,48},{80,64},{96,80},{112,96},{128,112},... | collective-permute-start | bytes 393224 | tf_op jit(solution)/shard_map/ppermute | solution.py:20
  36.7 6.3 %copy-start.6 = (f32[64]{0:T(128)S(1)}, f32[64]{0:T(128)}, u32[]{:S(2)}) copy-start(f32[64]{0:T(128)} %param.15) | copy-start | bytes 772
  267.9 85.4 %copy-start = (bf16[4,4,3,256,128]{4,3,2,1,0:T(8,128)(2,1)S(1)}, bf16[4,4,3,256,128]{4,3,2,1,0:T(8,128)(2,1)}, u32[]{:S(2)}) copy-start(bf16[4,4,3,256,128]{4,3,2,1,0:T(8,128)(2,1)} %get-tuple-element.11) | copy-start | bytes 9437188
  357.0 1.0 copy-start.2
  357.0 1.2 copy-start.3
  357.0 1.2 copy-start.9
  357.0 1.3 copy-start.10
Sparse Core Ops, SparseCore 0:
  247.6 105.5 all-reduce.1
